TPU v7x, 256 devices: a whole 4x4x8 slice. The times are simulated.
256 devices in a mesh: shot: 16 (over x_lo, y, core), rbin: 16 (over x_hi, z).
Axes of the slice: x: 4 (x_hi: 2, x_lo: 2; x = x_hi * 2 + x_lo), y: 4, z: 8, core: 2. Of those that a mesh axis runs over, the one named last changes fastest.
Arguments:
- local_gathers: bfloat16 [2, 2, 8192, 4096], P(None, None, 'shot', 'rbin'), may hold values from -6 to 6
- recorded_shots: bfloat16 [16, 2, 2, 1024, 2048], P('shot', None, None, 'rbin'), may hold values from -0.125 to 0.125
- block_owner: int32 [4], replicated, may hold values from 0 to 15, as said below
- aperture_start: int32 [8192], P('shot'), may hold values from 0 to 4095, as said below
- aperture_end: int32 [8192], P('shot'), may hold values from 1 to 4096
- taper_bin: int32 [4096], P('rbin'), may hold values from 0 to 7
- taper_gain: float32 [8], replicated, may hold values from 0.25 to 1
Outputs:
- multiples: float32 [2, 2048, 2, 8192], P(None, 'rbin', None, 'shot')
Inputs may be any that keep to these rules, and one draw needn't show every extreme that they name: `block_owner`: the 4 entries are distinct. aperture_start < aperture_end for every shot.
All inputs are finite; a program needn't handle non-finite values.
Results may differ from a plain program's by a relative error of at most 0.0029.
Values may be sent and summed in bfloat16 or wider, within the bound.
A program may use at most 128 MiB of HBM per device.

v0:
```python
import jax
import jax.numpy as jnp
from jax import lax
from jax.sharding import PartitionSpec as P

BLOCKS = 4
EDGE = 64


def from_root(value, axis, source):
    kept = jnp.where(lax.axis_index(axis) == source, value, 0).astype(value.dtype)
    return lax.psum(kept, axis)


def taper_weights(columns, aperture_start, aperture_end, taper_bin, taper_gain):
    inside = (columns[None, :] >= aperture_start[:, None]) & (
        columns[None, :] < aperture_end[:, None]
    )
    distance = jnp.minimum(
        columns[None, :] - aperture_start[:, None], aperture_end[:, None] - 1 - columns[None, :]
    )
    ramped = jnp.minimum((distance + 1).astype(jnp.float32) / EDGE, 1.0)
    labels = jnp.arange(taper_gain.shape[0], dtype=jnp.int32)
    bin_gain = jnp.sum(
        jnp.where(taper_bin[:, None] == labels[None, :], taper_gain[None, :], 0.0), axis=1
    )
    return jnp.where(inside, ramped, 0.0) * bin_gain[None, :]


def complex_rows(real_part, imag_part):
    upper_half = jnp.concatenate([real_part, -imag_part], axis=2)
    lower_half = jnp.concatenate([imag_part, real_part], axis=2)
    return jnp.concatenate([upper_half, lower_half], axis=1)


def per_device(
    local_gathers, recorded_shots, block_owner, aperture_start, aperture_end, taper_bin, taper_gain
):
    frequencies, _, shot_count, point_count = local_gathers.shape
    block_width = point_count // BLOCKS
    column_index = lax.axis_index("rbin")
    first_point = column_index * point_count
    columns = first_point + jnp.arange(point_count, dtype=jnp.int32)
    weight = taper_weights(columns, aperture_start, aperture_end, taper_bin, taper_gain)
    tapered = (local_gathers.astype(jnp.float32) * weight[None, None]).astype(jnp.bfloat16)
    own_slot = recorded_shots[0]
    grouped = tapered.reshape(frequencies, 2, shot_count, BLOCKS, block_width)

    def block_rows(block_index):
        return lax.dynamic_index_in_dim(grouped, block_index, 3, keepdims=False)

    out_columns = own_slot.shape[-1]
    accumulated = jnp.zeros((frequencies, out_columns, 2 * shot_count), jnp.float32)
    for position in range(BLOCKS):
        block_index = jnp.int32(position)
        root_device = block_owner[block_index]
        received = from_root(own_slot, "shot", root_device)
        operand = received.reshape(frequencies, -1, out_columns)

        def product(running, operand=operand, block_index=block_index):
            picked = block_rows(block_index)
            left_side = complex_rows(picked[:, 0], picked[:, 1])
            return running + lax.dot_general(
                operand, left_side, (((1,), (2,)), ((0,), (0,))), preferred_element_type=jnp.float32
            )

        accumulated = product(accumulated)
    accumulated = lax.psum_scatter(accumulated, "rbin", scatter_dimension=1, tiled=True)
    return -accumulated.reshape(frequencies, -1, 2, shot_count)


def solution(mesh):
    in_specs = (
        P(None, None, "shot", "rbin"),
        P("shot", None, None, "rbin", None),
        P(),
        P("shot"),
        P("shot"),
        P("rbin"),
        P(),
    )
    out_specs = P(None, "rbin", None, "shot")
    return jax.shard_map(
        per_device, mesh=mesh, in_specs=in_specs, out_specs=out_specs, check_vma=False
    )
```

profile of v0, /device:TPU:1, one launch (start us, length us, event | category | flops | bytes accessed | tf_op | source)
XLA Modules:
  0.0 503.2 jit_solution(17133983559959665374)
XLA Ops:
  6.5 0.0 copy-start.5
  6.5 0.0 copy-start.6
  6.5 0.0 copy-start.3
  6.5 0.0 copy-start.4
  6.5 0.0 all-reduce.3.cloned.1.call-start
  6.6 1.5 fusion.40
  10.5 2.5 broadcast_select_fusion
  13.0 2.3 copy.21
  15.3 1.3 copy.24
  16.6 1.3 copy.26
  17.9 1.3 copy.28
  19.2 0.0 all-reduce.3.cloned.1.call-update
  19.2 0.0 reduce-scatter.2.cloned.1.call-start
  19.3 1.5 copy.22
  20.8 0.0 copy-done.5
  20.8 0.0 copy-done.6
  20.8 0.1 select_reduce_fusion
  20.9 0.0 copy-done.3
  20.9 0.0 copy-done.4
  20.9 0.3 select_multiply_fusion
  21.2 0.2 multiply_convert_fusion
  21.4 0.1 fusion.39
  21.5 0.3 copy.30
  21.8 0.3 copy.31
  22.1 0.3 copy.32
  22.4 0.3 copy.33
  22.8 0.8 slice_bitcast_fusion.6
  23.7 133.8 %all-reduce.3.cloned.1.call-done = (bf16[2,128,2048]{1,2,0:T(8,128)(2,1)}, bf16[2,128,2048]{1,2,0:T(8,128)(2,1)}, bf16[2,128,2048]{1,2,0:T(8,128)(2,1)}, bf16[2,128,2048]{1,2,0:T(8,128)(2,1)}) async-done(((bf16[2,128,2048]{1,2,0:T(8,128)(2,1)}, bf16[2,128,2048]{1,2,0:T(8,128)(2,1)}, bf16[2,128,2048]{1,2,0:T(8,128)(2,1)}, bf16[2,128,2048]{1,2,0:T(8,128)(2,1)}), (bf16[2,128,2048]{1,2,0:T(8,128)(2,1)}, ...) | async-done | bytes 4194320 | tf_op jit(solution)/shard_map/psum | solution.py:12
  157.5 0.0 copy-start.2
  157.5 0.0 copy-start.1
  157.5 9.6 %fusion = f32[2,2048,1024]{2,1,0:T(8,128)} fusion(bf16[2,128,2048]{1,2,0:T(8,128)(2,1)} %get-tuple-element.6, bf16[2,512,64]{2,1,0:T(8,128)(2,1)} %get-tuple-element.22, bf16[2,512,64]{2,1,0:T(8,128)(2,1)S(1)} %get-tuple-element.21, bf16[2,512,64]{2,1,0:T(8,128)(2,1)S(1)} %fusion.35), kind=kOutput, calls=%fused_computation.6 | convolution fusion | flops 1075838976 | bytes 18219008 | tf_op jit(solution)/shard_map/dot_general | solution.py:63
  167.1 0.0 copy-done.2
  167.1 0.0 copy-start
  167.1 8.2 %fusion.8 = f32[2,2048,1024]{2,1,0:T(8,128)} fusion(bf16[2,128,2048]{1,2,0:T(8,128)(2,1)S(1)} %copy-done.2, bf16[2,512,64]{2,1,0:T(8,128)(2,1)S(1)} %get-tuple-element.20, bf16[2,512,64]{2,1,0:T(8,128)(2,1)S(1)} %get-tuple-element.19, bf16[2,512,64]{2,1,0:T(8,128)(2,1)S(1)} %fusion.36), kind=kOutput, calls=%fused_computation.14 | convolution fusion | flops 1075838976 | bytes 18219008 | tf_op jit(solution)/shard_map/dot_general | solution.py:63
  175.3 0.0 copy-done.1
  175.3 8.1 %fusion.16 = f32[2,2048,1024]{2,1,0:T(8,128)} fusion(bf16[2,128,2048]{1,2,0:T(8,128)(2,1)S(1)} %copy-done.1, bf16[2,512,64]{2,1,0:T(8,128)(2,1)S(1)} %get-tuple-element.24, bf16[2,512,64]{2,1,0:T(8,128)(2,1)S(1)} %get-tuple-element.23, bf16[2,512,64]{2,1,0:T(8,128)(2,1)S(1)} %fusion.37), kind=kOutput, calls=%fused_computation.22 | convolution fusion | flops 1075838976 | bytes 18219008 | tf_op jit(solution)/shard_map/dot_general | solution.py:63
  183.4 0.0 copy-done
  183.4 23.0 %add_add_fusion = f32[2,2048,1024]{2,1,0:T(8,128)} fusion(f32[2,2048,1024]{2,1,0:T(8,128)} %fusion.16, f32[2,2048,1024]{2,1,0:T(8,128)} %fusion, f32[2,2048,1024]{2,1,0:T(8,128)} %fusion.8, bf16[2,128,2048]{1,2,0:T(8,128)(2,1)S(1)} %copy-done, bf16[2,512,64]{2,1,0:T(8,128)(2,1)S(1)} %get-tuple-element.18, bf16[2,512,64]{2,1,0:T(8,128)(2,1)S(1)} %get-tuple-element.17, ...), kind=kOutput, calls=%fused_computation | convolution fusion | flops 1088421888 | bytes 68550656 | tf_op jit(solution)/shard_map/dot_general | solution.py:63
  206.5 0.0 reduce-scatter.2.cloned.1.call-update
  206.5 286.7 %reduce-scatter.2.cloned.1.call-done = f32[2,128,1024]{2,1,0:T(8,128)} async-done(((f32[2,2048,1024]{2,1,0:T(8,128)}), f32[2,128,1024]{2,1,0:T(8,128)}) %reduce-scatter.2.cloned.1.call-update) | async-done | bytes 1048592 | tf_op jit(solution)/shard_map/reduce_scatter | solution.py:68
  493.2 1.3 neg.22
  494.5 1.9 neg.23
  (9 shorter events, 0.3 us)
Async XLA Ops:
  6.5 14.2 %copy-start.5 = (s32[256]{0:T(256)S(1)}, s32[256]{0:T(256)}, u32[]{:S(2)}) copy-start(s32[256]{0:T(256)} %param.12) | copy-start | bytes 3076
  6.5 14.3 %copy-start.6 = (f32[8]{0:T(128)S(1)}, f32[8]{0:T(128)}, u32[]{:S(2)}) copy-start(f32[8]{0:T(128)} %param.13) | copy-start | bytes 100
  6.5 14.3 %copy-start.3 = (s32[512]{0:T(512)S(1)}, s32[512]{0:T(512)}, u32[]{:S(2)}) copy-start(s32[512]{0:T(512)} %param.11) | copy-start | bytes 6148
  6.5 14.4 %copy-start.4 = (s32[512]{0:T(512)S(1)}, s32[512]{0:T(512)}, u32[]{:S(2)}) copy-start(s32[512]{0:T(512)} %param.10) | copy-start | bytes 6148
  6.5 150.9 %all-reduce.3.cloned.1.call-start = ((), (), s32[]{:S(2)}) async-start(), calls=%async_computation.2 | async-start | bytes 8388608 | tf_op jit(solution)/shard_map/psum | solution.py:12
  19.2 474.0 %reduce-scatter.2.cloned.1.call-start = ((), (), s32[]{:S(2)}) async-start(), calls=%async_computation.1 | async-start | bytes 17825792 | tf_op jit(solution)/shard_map/reduce_scatter | solution.py:68
  157.5 9.7 %copy-start.2 = (bf16[2,128,2048]{1,2,0:T(8,128)(2,1)S(1)}, bf16[2,128,2048]{1,2,0:T(8,128)(2,1)}, u32[]{:S(2)}) copy-start(bf16[2,128,2048]{1,2,0:T(8,128)(2,1)} %get-tuple-element.7) | copy-start | bytes 3145732
  157.5 17.8 %copy-start.1 = (bf16[2,128,2048]{1,2,0:T(8,128)(2,1)S(1)}, bf16[2,128,2048]{1,2,0:T(8,128)(2,1)}, u32[]{:S(2)}) copy-start(bf16[2,128,2048]{1,2,0:T(8,128)(2,1)} %get-tuple-element.5) | copy-start | bytes 3145732
  167.1 16.3 %copy-start = (bf16[2,128,2048]{1,2,0:T(8,128)(2,1)S(1)}, bf16[2,128,2048]{1,2,0:T(8,128)(2,1)}, u32[]{:S(2)}) copy-start(bf16[2,128,2048]{1,2,0:T(8,128)(2,1)} %get-tuple-element.8) | copy-start | bytes 3145732
Sparse Core Ops, SparseCore 0:
  19.3 138.0 all-reduce.2
  206.6 286.5 reduce-scatter.1
where the time goes:
time: 503 us
  waiting for transfers between devices  420 us (83%)
  matrix products  49 us (10%)
  between operations  16 us (3%)
  local copies, waits for them, and re-layouts  13.1 us (3%)
    reduce_scatter x1, waiting for transfers between devices, per_device(): lax.psum_scatter(accumulated, 'rbin', scatter_dimension=1, tiled=True)  287 us
    psum x1, waiting for transfers between devices, from_root(): return lax.psum(kept, axis)  134 us
    dot_general x4, matrix products, product(): lax.dot_general(operand, left_side, (((1,), (2,)), ((0,), (0,))), preferr...  49 us
  transfers between devices with their start and end apart: 2, of which 2 were waited for; matrix products, arithmetic and copies ran while one was open for 1% of the time, Pallas kernels for 0%

commit v1 on v0

v1 whole, which is shorter than its diff:
```python
import jax
import jax.numpy as jnp
from jax import lax
from jax.experimental import pallas as pl
from jax.experimental.pallas import tpu as pltpu
from jax.sharding import PartitionSpec as P

BLOCKS = 4
EDGE = 64
FREQS = 2
Y = 4
SHOT = 16
Z = 8
LANES = 128
MESH = pl.DeviceIdType.MESH


def taper_weights(columns, aperture_start, aperture_end, taper_bin, taper_gain):
    inside = (columns[None, :] >= aperture_start[:, None]) & (
        columns[None, :] < aperture_end[:, None]
    )
    distance = jnp.minimum(
        columns[None, :] - aperture_start[:, None], aperture_end[:, None] - 1 - columns[None, :]
    )
    ramped = jnp.minimum((distance + 1).astype(jnp.float32) / EDGE, 1.0)
    labels = jnp.arange(taper_gain.shape[0], dtype=jnp.int32)
    bin_gain = jnp.sum(
        jnp.where(taper_bin[:, None] == labels[None, :], taper_gain[None, :], 0.0), axis=1
    )
    return jnp.where(inside, ramped, 0.0) * bin_gain[None, :]


def chain_length(sign, part):
    return 4 if (sign > 0) == (part == 0) else 3


def kernel(
    owner_ref, rec_ref, t_ref, out_ref,
    a2a_0, a2a_1, selx, A, tp, L, own, zsend, zrecv,
    a_loc, a_send, a_recv, g_send, g_recv, p_send, p_recv, ag_send, ag_recv, z_send, z_recv,
):
    a2a = (a2a_0, a2a_1)
    me = lax.axis_index("shot")
    rb = lax.axis_index("rbin")
    core = lax.rem(me, 2)
    q = lax.div(me, 2)
    x_lo = lax.div(q, Y)
    y = lax.rem(q, Y)
    x_hi = lax.div(rb, Z)
    z = lax.rem(rb, Z)
    half = t_ref.shape[3] * 4

    def shot_of(xl, yy, cc):
        return (xl * Y + lax.rem(yy, Y)) * 2 + cc

    partner = {"rbin": (1 - x_hi) * Z + z}
    z_next = {1: {"rbin": x_hi * Z + lax.rem(z + 1, Z)}, -1: {"rbin": x_hi * Z + lax.rem(z + Z - 1, Z)}}
    other_core = {"shot": shot_of(x_lo, y, 1 - core)}
    x_other = {"shot": shot_of(1 - x_lo, y, core)}
    y_up = {"shot": shot_of(x_lo, y + 1, core)}
    y_down = {"shot": shot_of(x_lo, y + Y - 1, core)}

    barrier = pltpu.get_barrier_semaphore()

    def greet(k, carry):
        pl.semaphore_signal(
            barrier, inc=1, device_id={"shot": lax.rem(me + k, SHOT)}, device_id_type=MESH
        )
        return carry

    lax.fori_loop(1, SHOT, greet, 0)
    for target in (partner, z_next[1], z_next[-1]):
        pl.semaphore_signal(barrier, inc=1, device_id=target, device_id_type=MESH)
    pl.semaphore_wait(barrier, SHOT - 1 + 3)

    pending = []

    def remote(src, dst, send_sem, recv_sem, target):
        copy = pltpu.make_async_remote_copy(
            src_ref=src, dst_ref=dst, send_sem=send_sem, recv_sem=recv_sem,
            device_id=target, device_id_type=MESH,
        )
        copy.start()
        pending.append(copy)

    def arrived(ref, sem):
        pltpu.make_async_copy(ref, ref, sem).wait()

    def chunk(f, target, h):
        start = pl.multiple_of(h * half + lax.div(target, 2) * LANES, LANES)
        return rec_ref.at[0, f, lax.rem(target, 2), :, pl.ds(start, LANES)]

    def exchange_start(f):
        def body(k, carry):
            target = lax.rem(me + k, SHOT)
            for h in range(2):
                pltpu.make_async_remote_copy(
                    src_ref=chunk(f, target, h), dst_ref=a2a[f].at[me, h],
                    send_sem=a_send.at[f, h, k], recv_sem=a_recv.at[f, h, k],
                    device_id={"shot": target}, device_id_type=MESH,
                ).start()
            return carry

        lax.fori_loop(1, SHOT, body, 0)
        for h in range(2):
            pltpu.make_async_copy(chunk(f, me, h), a2a[f].at[me, h], a_loc.at[f, h]).start()

    def exchange_wait(f):
        def body(k, carry):
            source = lax.rem(me + SHOT - k, SHOT)
            for h in range(2):
                arrived(a2a[f].at[source, h], a_recv.at[f, h, k])
            return carry

        lax.fori_loop(1, SHOT, body, 0)
        for h in range(2):
            arrived(a2a[f].at[me, h], a_loc.at[f, h])

    def exchange_end(f):
        def body(k, carry):
            target = lax.rem(me + k, SHOT)
            for h in range(2):
                arrived(a2a[f].at[target, h], a_send.at[f, h, k])
            return carry

        lax.fori_loop(1, SHOT, body, 0)

    def gathers_start(f):
        remote(t_ref.at[f], tp.at[f], g_send.at[f], g_recv.at[f], partner)

    def select(f):
        for k in range(BLOCKS):
            owner = owner_ref[k]
            rows = pl.ds((k % 2) * 64, 64)
            selx[f, k // 2, rows, :] = a2a[f][owner, 1 - x_hi]
            A[f, q, core, 0, k // 2, rows, :] = a2a[f][owner, x_hi]
        remote(selx.at[f], A.at[f, q, core, 1], p_send.at[f], p_recv.at[f], partner)

    def at_chip(xl, yy):
        return xl * Y + lax.rem(yy, Y)

    pieces = [
        at_chip(1 - x_lo, y),
        at_chip(x_lo, y + Y - 1),
        at_chip(1 - x_lo, y + Y - 1),
        at_chip(x_lo, y + 1),
        at_chip(1 - x_lo, y + 1),
        at_chip(x_lo, y + 2),
        at_chip(1 - x_lo, y + 2),
    ]

    def ag_copy(f, b, index, piece, target):
        ref = A.at[f, piece, core, b]
        remote(ref, ref, ag_send.at[f, b, index], ag_recv.at[f, b, index], target)

    def ag_got(f, b, index):
        arrived(A.at[f, pieces[index], core, b], ag_recv.at[f, b, index])
        ag_copy(f, b, 8 + index, pieces[index], other_core)

    def ag_first(f, b):
        ag_copy(f, b, 0, q, x_other)
        ag_copy(f, b, 1, q, y_up)
        ag_copy(f, b, 3, q, y_down)
        ag_copy(f, b, 7, q, other_core)

    def ag_begin(f):
        ag_first(f, 0)
        arrived(A.at[f, q, core, 1], p_recv.at[f])
        ag_first(f, 1)

    def ag_second(f):
        for b in range(2):
            ag_got(f, b, 0)
            ag_copy(f, b, 2, pieces[0], y_up)
            ag_copy(f, b, 4, pieces[0], y_down)

    def ag_relay(f):
        for b in range(2):
            ag_got(f, b, 1)
            ag_copy(f, b, 5, pieces[1], y_up)
            ag_got(f, b, 4)
            ag_copy(f, b, 6, pieces[4], y_down)
            ag_got(f, b, 3)
            ag_got(f, b, 2)

    def ag_finish(f):
        for b in range(2):
            ag_got(f, b, 5)
            ag_got(f, b, 6)
        for b in range(2):
            arrived(A.at[f, q, 1 - core, b], ag_recv.at[f, b, 7])
            for index in range(7):
                arrived(A.at[f, pieces[index], 1 - core, b], ag_recv.at[f, b, 8 + index])

    width = t_ref.shape[3]

    def lhs(f):
        arrived(tp.at[f], g_recv.at[f])
        for b, ref in enumerate((t_ref, tp)):
            cols = [pl.ds(c * 2 * width + b * width, width) for c in range(2)]
            L[0, :, cols[0]] = ref[f, 0]
            L[0, :, cols[1]] = -ref[f, 1]
            L[1, :, cols[0]] = ref[f, 1]
            L[1, :, cols[1]] = ref[f, 0]

    def z_put(f, sign, part, step):
        i = 0 if sign > 0 else 1
        remote(
            zsend.at[f, i, part, step], zrecv.at[f, i, part, step],
            z_send.at[f, i, part, step], z_recv.at[f, i, part, step], z_next[sign],
        )

    def product(f, pair):
        right = jnp.concatenate(
            [A[f, lax.rem(z + d + Z, Z)].reshape(-1, LANES) for d in pair], axis=1
        )
        for part in range(2):
            value = jnp.dot(L[part], right, preferred_element_type=jnp.float32)
            for n, d in enumerate(pair):
                own[f, d % Z, part] = value[:, n * LANES:(n + 1) * LANES]

    def z_open(f):
        lhs(f)
        product(f, (4, 3))
        z_first(f, 1, 0)
        z_first(f, -1, 1)
        z_first(f, 1, 1)
        product(f, (-3, 2))
        z_first(f, -1, 0)
        product(f, (-2, 1))
        product(f, (-1, 0))

    def z_first(f, sign, part):
        i = 0 if sign > 0 else 1
        d = sign * chain_length(sign, part)
        zsend[f, i, part, 0] = own[f, d % Z, part].astype(jnp.bfloat16)
        z_put(f, sign, part, 0)

    def z_step(f, step):
        for sign, part in ((1, 0), (-1, 1), (1, 1), (-1, 0)):
            length = chain_length(sign, part)
            if step >= length:
                continue
            i = 0 if sign > 0 else 1
            arrived(zrecv.at[f, i, part, step - 1], z_recv.at[f, i, part, step - 1])
            d = sign * (length - step)
            zsend[f, i, part, step] = (
                zrecv[f, i, part, step - 1].astype(jnp.float32) + own[f, d % Z, part]
            ).astype(jnp.bfloat16)
            z_put(f, sign, part, step)

    def z_last(f):
        for part in range(2):
            total = own[f, 0, part]
            for i, sign in enumerate((1, -1)):
                last = chain_length(sign, part) - 1
                arrived(zrecv.at[f, i, part, last], z_recv.at[f, i, part, last])
                total = total + zrecv[f, i, part, last].astype(jnp.float32)
            out_ref[f, part] = total.T

    exchange_start(0)
    gathers_start(0)
    exchange_start(1)
    gathers_start(1)
    exchange_wait(0)
    select(0)
    ag_begin(0)
    ag_second(0)
    ag_relay(0)
    exchange_wait(1)
    select(1)
    ag_finish(0)
    z_open(0)
    ag_begin(1)
    z_step(0, 1)
    ag_second(1)
    z_step(0, 2)
    ag_relay(1)
    ag_finish(1)
    z_step(0, 3)
    z_open(1)
    z_last(0)
    for step in range(1, 4):
        z_step(1, step)
    z_last(1)
    for f in range(FREQS):
        exchange_end(f)
    for copy in pending:
        copy.wait_send()


def convolve(owner, recorded, tapered):
    freqs, _, shots, width = tapered.shape
    bf16, f32, dma = jnp.bfloat16, jnp.float32, pltpu.SemaphoreType.DMA
    return pl.pallas_call(
        kernel,
        out_shape=jax.ShapeDtypeStruct((freqs, 2, LANES, shots), f32),
        in_specs=[
            pl.BlockSpec(memory_space=pltpu.SMEM),
            pl.BlockSpec(memory_space=pl.ANY),
            pl.BlockSpec(memory_space=pltpu.VMEM),
        ],
        out_specs=pl.BlockSpec(memory_space=pltpu.VMEM),
        scratch_shapes=[
            pltpu.VMEM((SHOT, 2, 64, LANES), bf16),
            pltpu.VMEM((SHOT, 2, 64, LANES), bf16),
            pltpu.VMEM((freqs, 2, LANES, LANES), bf16),
            pltpu.VMEM((freqs, Z, 2, 2, 2, LANES, LANES), bf16),
            pltpu.VMEM((freqs, 2, shots, width), bf16),
            pltpu.VMEM((2, shots, 4 * width), bf16),
            pltpu.VMEM((freqs, Z, 2, shots, LANES), f32),
            pltpu.VMEM((freqs, 2, 2, 4, shots, LANES), bf16),
            pltpu.VMEM((freqs, 2, 2, 4, shots, LANES), bf16),
            dma((freqs, 2)),
            dma((freqs, 2, SHOT)),
            dma((freqs, 2, SHOT)),
            dma((freqs,)),
            dma((freqs,)),
            dma((freqs,)),
            dma((freqs,)),
            dma((freqs, 2, 15)),
            dma((freqs, 2, 15)),
            dma((freqs, 2, 2, 4)),
            dma((freqs, 2, 2, 4)),
        ],
        compiler_params=pltpu.CompilerParams(
            collective_id=0, has_side_effects=True, vmem_limit_bytes=48 * 1024 * 1024
        ),
        name="convolve",
    )(owner, recorded, tapered)


def per_device(
    local_gathers, recorded_shots, block_owner, aperture_start, aperture_end, taper_bin, taper_gain
):
    point_count = local_gathers.shape[3]
    columns = lax.axis_index("rbin") * point_count + jnp.arange(point_count, dtype=jnp.int32)
    weight = taper_weights(columns, aperture_start, aperture_end, taper_bin, taper_gain)
    tapered = -(local_gathers.astype(jnp.float32) * weight[None, None]).astype(jnp.bfloat16)
    return convolve(block_owner, recorded_shots, tapered).transpose(0, 2, 1, 3)


def solution(mesh):
    in_specs = (
        P(None, None, "shot", "rbin"),
        P("shot", None, None, "rbin", None),
        P(),
        P("shot"),
        P("shot"),
        P("rbin"),
        P(),
    )
    out_specs = P(None, "rbin", None, "shot")
    return jax.shard_map(
        per_device, mesh=mesh, in_specs=in_specs, out_specs=out_specs, check_vma=False
    )
```

time: 503 us -> 116 us (0.23)
  waiting for transfers between devices: 420 us -> 0 us
  Pallas kernels: 0 us -> 110 us
  matrix products: 49 us -> 0 us
  between operations: 16 us -> 0.05 us
  local copies, waits for them, and re-layouts: 13.1 us -> 1.79 us
    reduce_scatter x1 -> x0, waiting for transfers between devices: 287 us -> none  [per_device(): lax.psum_scatter(accumulated, 'rbin', scatter_dimension=1, tiled=True)]
    psum x1 -> x0, waiting for transfers between devices: 134 us -> none  [from_root(): return lax.psum(kept, axis)]
    pallas_call x0 -> x1, Pallas kernels: none -> 110 us  [convolve(): pl.pallas_call(kernel, out_shape=jax.ShapeDtypeStruct((freqs, 2, LANES, s...]
    dot_general x4 -> x0, matrix products: 49 us -> none  [product(): lax.dot_general(operand, left_side, (((1,), (2,)), ((0,), (0,))), preferr...]
    reshape x4 -> x0, local copies, waits for them, and re-layouts: 6.21 us -> none  [per_device(): operand = received.reshape(frequencies, -1, out_columns)]
  transfers between devices with their start and end apart: 2 -> 0, of which waited for: 2 -> 0; matrix products, arithmetic and copies ran while one was open for 1% -> 0% of each run, Pallas kernels for 0% -> 0%
where the time goes in v1:
time: 116 us
  Pallas kernels  110 us (95%)
  other arithmetic  4.05 us (3%)
  local copies, waits for them, and re-layouts  1.79 us (2%)
    pallas_call x1, Pallas kernels, convolve(): pl.pallas_call(kernel, out_shape=jax.ShapeDtypeStruct((freqs, 2, LANES, s...  110 us

profile of v1, /device:TPU:1, one launch (start us, length us, event | category | flops | bytes accessed | tf_op | source)
XLA Modules:
  0.0 115.7 jit_solution(13394730731727564347)
XLA Ops:
  0.0 0.8 select_reduce_fusion
  0.8 0.7 broadcast_add_fusion
  1.5 1.0 select_multiply_fusion
  2.5 0.0 copy-start
  2.5 0.0 copy-start.1
  2.5 1.6 %fusion.t_ref = bf16[2,2,512,256]{3,2,1,0:T(8,128)(2,1)S(1)} fusion(bf16[2,2,512,256]{3,2,1,0:T(8,128)(2,1)} %param.7, f32[512,256]{1,0:T(8,128)S(1)} %select_multiply_fusion), kind=kLoop, calls=%fused_computation.1 | loop fusion | flops 2097152 | bytes 2621440 | tf_op jit(solution)/shard_map/neg | solution.py:339
  4.1 0.0 copy-done
  4.1 0.0 copy-done.1
  4.1 109.9 %convolve.1 = f32[2,2,128,512]{3,2,1,0:T(8,128)S(1)} custom-call(s32[4]{0:T(128)S(1)} %copy-done.1, bf16[1,2,2,64,2048]{4,3,2,1,0:T(8,128)(2,1)S(1)} %copy-done, bf16[2,2,512,256]{3,2,1,0:T(8,128)(2,1)S(1)} %fusion.t_ref), custom_call_target="tpu_custom_call" | custom-call | tf_op jit(solution)/shard_map/convolve/pallas_call | solution.py:295
  114.0 1.8 %copy.9 = f32[2,128,2,512]{3,2,1,0:T(2,128)} copy(f32[2,128,2,512]{3,1,2,0:T(8,128)S(1)} %bitcast.1) | data formatting | bytes 2097152 | tf_op jit(solution)/shard_map/transpose | solution.py:340
  (1 shorter events, 0.0 us)
Async XLA Ops:
  2.5 1.6 %copy-start = (bf16[1,2,2,64,2048]{4,3,2,1,0:T(8,128)(2,1)S(1)}, bf16[1,2,2,64,2048]{4,3,2,1,0:T(8,128)(2,1)}, u32[]{:S(2)}) copy-start(bf16[1,2,2,64,2048]{4,3,2,1,0:T(8,128)(2,1)} %rec_ref.1) | copy-start | bytes 3145732
  2.5 1.6 %copy-start.1 = (s32[4]{0:T(128)S(1)}, s32[4]{0:T(128)}, u32[]{:S(2)}) copy-start(s32[4]{0:T(128)} %owner_ref.1) | copy-start | bytes 52

commit v2 on v1

--- a/solution.py
+++ b/solution.py
@@ -260,24 +260,24 @@
 
     exchange_start(0)
     gathers_start(0)
-    exchange_start(1)
-    gathers_start(1)
     exchange_wait(0)
     select(0)
     ag_begin(0)
+    exchange_start(1)
     ag_second(0)
     ag_relay(0)
+    gathers_start(1)
+    ag_finish(0)
+    z_open(0)
     exchange_wait(1)
     select(1)
-    ag_finish(0)
-    z_open(0)
+    z_step(0, 1)
     ag_begin(1)
-    z_step(0, 1)
     ag_second(1)
     z_step(0, 2)
     ag_relay(1)
+    z_step(0, 3)
     ag_finish(1)
-    z_step(0, 3)
     z_open(1)
     z_last(0)
     for step in range(1, 4):

time: 116 us -> 102 us (0.88)
  Pallas kernels: 110 us -> 96.3 us
    pallas_call x1, Pallas kernels: 110 us -> 96.3 us  [convolve(): pl.pallas_call(kernel, out_shape=jax.ShapeDtypeStruct((freqs, 2, LANES, s...]
where the time goes in v2:
time: 102 us
  Pallas kernels  96.3 us (94%)
  other arithmetic  4.05 us (4%)
  local copies, waits for them, and re-layouts  1.79 us (2%)
    pallas_call x1, Pallas kernels, convolve(): pl.pallas_call(kernel, out_shape=jax.ShapeDtypeStruct((freqs, 2, LANES, s...  96.3 us

profile of v2, /device:TPU:1, one launch (start us, length us, event | category | flops | bytes accessed | tf_op | source)
XLA Modules:
  0.0 102.2 jit_solution(9212107030829931669)
XLA Ops:
  0.0 0.8 select_reduce_fusion
  0.8 0.7 broadcast_add_fusion
  1.5 1.0 select_multiply_fusion
  2.5 0.0 copy-start
  2.5 0.0 copy-start.1
  2.5 1.6 %fusion.t_ref = bf16[2,2,512,256]{3,2,1,0:T(8,128)(2,1)S(1)} fusion(bf16[2,2,512,256]{3,2,1,0:T(8,128)(2,1)} %param.7, f32[512,256]{1,0:T(8,128)S(1)} %select_multiply_fusion), kind=kLoop, calls=%fused_computation.1 | loop fusion | flops 2097152 | bytes 2621440 | tf_op jit(solution)/shard_map/neg | solution.py:339
  4.1 0.0 copy-done
  4.1 0.0 copy-done.1
  4.1 96.3 %convolve.1 = f32[2,2,128,512]{3,2,1,0:T(8,128)S(1)} custom-call(s32[4]{0:T(128)S(1)} %copy-done.1, bf16[1,2,2,64,2048]{4,3,2,1,0:T(8,128)(2,1)S(1)} %copy-done, bf16[2,2,512,256]{3,2,1,0:T(8,128)(2,1)S(1)} %fusion.t_ref), custom_call_target="tpu_custom_call" | custom-call | tf_op jit(solution)/shard_map/convolve/pallas_call | solution.py:295
  100.5 1.8 %copy.9 = f32[2,128,2,512]{3,2,1,0:T(2,128)} copy(f32[2,128,2,512]{3,1,2,0:T(8,128)S(1)} %bitcast.1) | data formatting | bytes 2097152 | tf_op jit(solution)/shard_map/transpose | solution.py:340
  (1 shorter events, 0.0 us)
Async XLA Ops:
  2.5 1.6 %copy-start = (bf16[1,2,2,64,2048]{4,3,2,1,0:T(8,128)(2,1)S(1)}, bf16[1,2,2,64,2048]{4,3,2,1,0:T(8,128)(2,1)}, u32[]{:S(2)}) copy-start(bf16[1,2,2,64,2048]{4,3,2,1,0:T(8,128)(2,1)} %rec_ref.1) | copy-start | bytes 3145732
  2.5 1.6 %copy-start.1 = (s32[4]{0:T(128)S(1)}, s32[4]{0:T(128)}, u32[]{:S(2)}) copy-start(s32[4]{0:T(128)} %owner_ref.1) | copy-start | bytes 52
